TPU v7x, 512 devices: a whole 4x4x16 slice. The times are simulated.
512 devices in a mesh: gx: 16 (over z), gy: 4 (over x), gz: 8 (over y, core).
Axes of the slice: x: 4, y: 4, z: 16, core: 2. Of those that a mesh axis runs over, the one named last changes fastest.
Arguments:
- flow: float32 [4, 128, 64, 1024], P(None, 'gx', 'gy', 'gz'), may hold values from -3 to 3
- basis: float32 [127, 3, 131072], P(None, None, ('gx', 'gy', 'gz')), may hold values from -1150 to 1150
- sample: int32 [131072], P(('gx', 'gy', 'gz')), may hold values from 0 to 16383
Outputs:
- flow_next: float32 [4, 128, 64, 1024], P(None, 'gx', 'gy', 'gz')
- basis_next: float32 [128, 3, 131072], P(None, None, ('gx', 'gy', 'gz'))
- factor: float32 [128, 128], replicated
All inputs are finite; a program needn't handle non-finite values.
Results may differ from a plain program's by a relative error of at most 0.000065.
Values sent between devices are 32-bit elements; how exact they have to be, the bound alone decides.
A program may use at most 64 MiB of HBM per device.

v0:
```python
import jax
import jax.numpy as jnp
from jax import lax
from jax.sharding import PartitionSpec as P

DT_STEP = 0.35
VISCOSITY = 0.2
SOUND_SQ = 1.0
DRIVING = 0.5


def padded(block, sides, width, periodic):
    for axis, dim in sides:
        count = lax.axis_size(axis)
        forward = [(i, i + 1) for i in range(count - 1)]
        if periodic:
            forward.append((count - 1, 0))
        backward = [(target, source) for source, target in forward]
        low = lax.ppermute(
            lax.slice_in_dim(block, block.shape[dim] - width, None, axis=dim), axis, forward
        )
        high = lax.ppermute(lax.slice_in_dim(block, 0, width, axis=dim), axis, backward)
        block = jnp.concatenate([low, block, high], axis=dim)
    return block


def rates(ext):
    centre = ext[:, 1:-1, 1:-1, 1:-1]
    x_plus = ext[:, 2:, 1:-1, 1:-1]
    x_minus = ext[:, :-2, 1:-1, 1:-1]
    y_plus = ext[:, 1:-1, 2:, 1:-1]
    y_minus = ext[:, 1:-1, :-2, 1:-1]
    z_plus = ext[:, 1:-1, 1:-1, 2:]
    z_minus = ext[:, 1:-1, 1:-1, :-2]
    slope_x = 0.5 * (x_plus - x_minus)
    slope_y = 0.5 * (y_plus - y_minus)
    slope_z = 0.5 * (z_plus - z_minus)
    laplace = x_plus + x_minus + (y_plus + y_minus) + (z_plus + z_minus) - 6.0 * centre
    advect = centre[0] * slope_x[:3] + centre[1] * slope_y[:3] + centre[2] * slope_z[:3]
    pressure = jnp.stack([slope_x[3], slope_y[3], slope_z[3]])
    forcing = jnp.array([DRIVING, 0.0, 0.0], dtype=jnp.float32).reshape(3, 1, 1, 1)
    velocity = VISCOSITY * laplace[:3] - advect - pressure + forcing
    density = -SOUND_SQ * (slope_x[0] + slope_y[1] + slope_z[2])
    return jnp.concatenate([velocity, density[None]], axis=0)


def extend_one(fields):
    walled = padded(fields, (("gy", 2),), 1, False)
    return padded(walled, (("gx", 1), ("gz", 3)), 1, True)


def local(flow, basis, sample):
    points = basis.shape[2]
    modes = basis.shape[0]
    count = 3.0 * points * lax.axis_size("gx") * lax.axis_size("gy") * lax.axis_size("gz")
    section_one = flow + DT_STEP * rates(extend_one(flow))
    section_two = 0.75 * flow + 0.25 * (section_one + DT_STEP * rates(extend_one(section_one)))
    flow_next = 1.0 / 3.0 * flow + 2.0 / 3.0 * (
        section_two + DT_STEP * rates(extend_one(section_two))
    )
    velocity = flow_next[:3].reshape(3, -1)
    snapshot = jnp.take(velocity, sample, axis=1)
    stacked = jnp.concatenate([basis, snapshot[None]], axis=0).reshape(modes + 1, 3 * points)
    local_gram = jnp.dot(
        stacked, stacked.T, precision=lax.Precision.HIGHEST, preferred_element_type=jnp.float32
    )
    gram = lax.psum(local_gram, ("gx", "gy", "gz")) / count
    lower = jnp.linalg.cholesky(gram)
    basis_next = jax.scipy.linalg.solve_triangular(lower, stacked, lower=True).reshape(
        modes + 1, 3, points
    )
    return (flow_next, basis_next, lower.T)


def solution(mesh):
    return jax.shard_map(
        local,
        mesh=mesh,
        in_specs=(
            P(None, "gx", "gy", "gz"),
            P(None, None, ("gx", "gy", "gz")),
            P(("gx", "gy", "gz")),
        ),
        out_specs=(P(None, "gx", "gy", "gz"), P(None, None, ("gx", "gy", "gz")), P()),
        check_vma=False,
    )
```

profile of v0, /device:TPU:1, one launch (start us, length us, event | category | flops | bytes accessed | tf_op | source)
XLA Modules:
  0.0 582.4 jit_solution(7620865436270588193)
XLA Ops:
  8.3 3.9 collective-permute-start
  12.2 1.3 collective-permute-start.1
  14.4 2.2 collective-permute-done.1
  17.5 11.1 %collective-permute-start.2 = (f32[4,1,18,128]{3,2,1,0:T(8,128)S(1)}, f32[4,1,18,128]{3,2,1,0:T(8,128)S(1)}, u32[]{:S(2)}, u32[]{:S(2)}) collective-permute-start(f32[4,1,18,128]{3,2,1,0:T(8,128)S(1)} %get-tuple-element.41), channel_id=1, source_target_pairs={{32,0},{64,32},{96,64},{128,96},{160,128},{192,160},{224,192},{256... | collective-permute-start | bytes 110600 | tf_op jit(solution)/shard_map/ppermute | solution.py:22
  28.6 1.9 collective-permute-start.3
  31.2 3.4 collective-permute-done.3
  35.9 3.5 collective-permute-start.4
  40.6 1.6 subtract_multiply_fusion.5
  42.2 5.2 collective-permute-done.4
  47.4 1.4 subtract_multiply_fusion.4
  48.9 1.5 fusion.24
  50.4 3.1 collective-permute-start.6
  53.6 1.3 collective-permute-start.7
  54.9 3.1 collective-permute-done.7
  58.1 1.9 collective-permute-start.8
  60.0 3.4 collective-permute-start.9
  63.4 2.6 collective-permute-done.9
  66.3 4.2 collective-permute-start.10
  70.7 6.5 %collective-permute-done.10 = f32[4,10,18,1]{3,2,1,0:T(8,128)S(1)} collective-permute-done((f32[4,10,18,1]{3,2,1,0:T(8,128)S(1)}, f32[4,10,18,1]{3,2,1,0:T(8,128)S(1)}, u32[]{:S(2)}, u32[]{:S(2)}) %collective-permute-start.10) | collective-permute-done | bytes 2912 | tf_op jit(solution)/shard_map/ppermute | solution.py:22
  77.9 2.8 collective-permute-start.12
  80.7 1.3 collective-permute-start.13
  82.2 3.0 collective-permute-done.13
  85.2 1.9 collective-permute-start.14
  87.1 3.5 collective-permute-start.15
  90.7 2.5 collective-permute-done.15
  93.4 5.4 collective-permute-start.16
  99.0 5.4 collective-permute-done.16
  105.3 4.7 copy.16
  110.1 4.1 gather_fusion
  115.8 433.0 %all-reduce.2.cloned.1.call-done = f32[128,128]{0,1:T(8,128)} async-done(((f32[128,128]{0,1:T(8,128)}), f32[128,128]{0,1:T(8,128)}) %all-reduce.2.cloned.1.call-update) | async-done | bytes 65552 | tf_op jit(solution)/shard_map/psum | solution.py:67
  550.6 11.7 %cholesky.16 = f32[128,128]{1,0:T(8,128)S(1)} custom-call(f32[128,128]{1,0:T(8,128)S(1)} %fusion.57), custom_call_target="Cholesky" | custom-call | tf_op jit(solution)/shard_map/jit(cholesky)/cholesky | solution.py:68
  563.7 9.8 %custom-call.7 = f32[1,128,128]{1,2,0:T(8,128)S(1)} custom-call(f32[1,128,128]{2,1,0:T(8,128)S(1)} %get-tuple-element.70), custom_call_target="InvertDiagBlocksLowerTriangular" | custom-call | tf_op jit(solution)/shard_map/jit(_solve_triangular)/triangular_solve | solution.py:69
  (71 shorter events, 15.2 us)
Async XLA Ops:
  7.2 43.2 %copy-start = (f32[4,8,16,128]{3,2,1,0:T(8,128)S(1)}, f32[4,8,16,128]{3,2,1,0:T(8,128)}, u32[]{:S(2)}) copy-start(f32[4,8,16,128]{3,2,1,0:T(8,128)} %param.6) | copy-start | bytes 786436
  7.2 47.7 %copy-start.4 = (s32[256]{0:T(256)S(1)}, s32[256]{0:T(256)}, u32[]{:S(2)}) copy-start(s32[256]{0:T(256)} %param.8) | copy-start | bytes 3076
  7.2 541.6 %all-reduce.2.cloned.1.call-start = ((), (), s32[]{:S(2)}) async-start(), calls=%async_computation | async-start | bytes 131072 | tf_op jit(solution)/shard_map/psum | solution.py:67
  8.3 6.2 %collective-permute-start = (f32[4,8,1,128]{3,2,1,0:T(1,128)S(1)}, f32[4,8,1,128]{3,2,1,0:T(1,128)S(1)}, u32[]{:S(2)}, u32[]{:S(2)}) collective-permute-start(f32[4,8,1,128]{3,2,1,0:T(1,128)S(1)} %get-tuple-element.67), channel_id=1, source_target_pairs={{0,8},{8,16},{16,24},{1,9},{9,17},{17,25},{2,10},{10,18},{18,26},{... | collective-permute-start | bytes 49160 | tf_op jit(solution)/shard_map/ppermute | solution.py:19
  12.2 4.5 collective-permute-start.1
  17.5 13.7 %collective-permute-start.2 = (f32[4,1,18,128]{3,2,1,0:T(8,128)S(1)}, f32[4,1,18,128]{3,2,1,0:T(8,128)S(1)}, u32[]{:S(2)}, u32[]{:S(2)}) collective-permute-start(f32[4,1,18,128]{3,2,1,0:T(8,128)S(1)} %get-tuple-element.41), channel_id=1, source_target_pairs={{32,0},{64,32},{96,64},{128,96},{160,128},{192,160},{224,192},{256... | collective-permute-start | bytes 110600 | tf_op jit(solution)/shard_map/ppermute | solution.py:22
  28.6 6.0 %collective-permute-start.3 = (f32[4,1,18,128]{3,2,1,0:T(8,128)S(1)}, f32[4,1,18,128]{3,2,1,0:T(8,128)S(1)}, u32[]{:S(2)}, u32[]{:S(2)}) collective-permute-start(f32[4,1,18,128]{3,2,1,0:T(8,128)S(1)} %get-tuple-element.40), channel_id=1, source_target_pairs={{0,32},{32,64},{64,96},{96,128},{128,160},{160,192},{192,224},{224... | collective-permute-start | bytes 110600 | tf_op jit(solution)/shard_map/ppermute | solution.py:19
  35.7 41.9 %copy-start.3 = (f32[3]{0:T(128)S(1)}, f32[3]{0:T(128)}, u32[]{:S(2)}) copy-start(f32[3]{0:T(128)} %constant.80.clone) | copy-start | bytes 40
  35.9 11.5 %collective-permute-start.4 = (f32[4,10,18,1]{3,2,1,0:T(8,128)S(1)}, f32[4,10,18,1]{3,2,1,0:T(8,128)S(1)}, u32[]{:S(2)}, u32[]{:S(2)}) collective-permute-start(f32[4,10,18,1]{3,2,1,0:T(8,128)S(1)} %get-tuple-element.31), channel_id=1, source_target_pairs={{1,0},{2,1},{3,2},{4,3},{5,4},{6,5},{7,6},{0,7},{9,8},{10,9},{11,1... | collective-permute-start | bytes 8648 | tf_op jit(solution)/shard_map/ppermute | solution.py:22
  39.4 8.0 %collective-permute-start.5 = (f32[4,10,18,1]{3,2,1,0:T(8,128)S(1)}, f32[4,10,18,1]{3,2,1,0:T(8,128)S(1)}, u32[]{:S(2)}, u32[]{:S(2)}) collective-permute-start(f32[4,10,18,1]{3,2,1,0:T(8,128)S(1)} %get-tuple-element.32), channel_id=1, source_target_pairs={{0,1},{1,2},{2,3},{3,4},{4,5},{5,6},{6,7},{7,0},{8,9},{9,10},{10,1... | collective-permute-start | bytes 8648 | tf_op jit(solution)/shard_map/ppermute | solution.py:19
  42.2 39.8 %copy-start.1 = (f32[127,3,256]{2,0,1:T(8,128)S(1)}, f32[127,3,256]{2,0,1:T(8,128)}, u32[]{:S(2)}) copy-start(f32[127,3,256]{2,0,1:T(8,128)} %param.7) | copy-start | bytes 1170436
  50.4 4.5 collective-permute-start.6
  53.6 4.5 collective-permute-start.7
  58.1 5.3 collective-permute-start.8
  60.0 6.0 %collective-permute-start.9 = (f32[4,1,18,128]{3,2,1,0:T(8,128)S(1)}, f32[4,1,18,128]{3,2,1,0:T(8,128)S(1)}, u32[]{:S(2)}, u32[]{:S(2)}) collective-permute-start(f32[4,1,18,128]{3,2,1,0:T(8,128)S(1)} %get-tuple-element.37), channel_id=1, source_target_pairs={{0,32},{32,64},{64,96},{96,128},{128,160},{160,192},{192,224},{224... | collective-permute-start | bytes 110600 | tf_op jit(solution)/shard_map/ppermute | solution.py:19
  66.3 10.9 %collective-permute-start.10 = (f32[4,10,18,1]{3,2,1,0:T(8,128)S(1)}, f32[4,10,18,1]{3,2,1,0:T(8,128)S(1)}, u32[]{:S(2)}, u32[]{:S(2)}) collective-permute-start(f32[4,10,18,1]{3,2,1,0:T(8,128)S(1)} %get-tuple-element.29), channel_id=1, source_target_pairs={{1,0},{2,1},{3,2},{4,3},{5,4},{6,5},{7,6},{0,7},{9,8},{10,9},{11,1... | collective-permute-start | bytes 8648 | tf_op jit(solution)/shard_map/ppermute | solution.py:22
  70.5 6.6 %collective-permute-start.11 = (f32[4,10,18,1]{3,2,1,0:T(8,128)S(1)}, f32[4,10,18,1]{3,2,1,0:T(8,128)S(1)}, u32[]{:S(2)}, u32[]{:S(2)}) collective-permute-start(f32[4,10,18,1]{3,2,1,0:T(8,128)S(1)} %get-tuple-element.30), channel_id=1, source_target_pairs={{0,1},{1,2},{2,3},{3,4},{4,5},{5,6},{6,7},{7,0},{8,9},{9,10},{10,1... | collective-permute-start | bytes 8648 | tf_op jit(solution)/shard_map/ppermute | solution.py:19
  77.9 4.3 collective-permute-start.12
  80.7 4.5 collective-permute-start.13
  85.2 5.5 collective-permute-start.14
  87.1 6.0 %collective-permute-start.15 = (f32[4,1,18,128]{3,2,1,0:T(8,128)S(1)}, f32[4,1,18,128]{3,2,1,0:T(8,128)S(1)}, u32[]{:S(2)}, u32[]{:S(2)}) collective-permute-start(f32[4,1,18,128]{3,2,1,0:T(8,128)S(1)} %get-tuple-element.34), channel_id=1, source_target_pairs={{0,32},{32,64},{64,96},{96,128},{128,160},{160,192},{192,224},{224... | collective-permute-start | bytes 110600 | tf_op jit(solution)/shard_map/ppermute | solution.py:19
  93.4 11.0 %collective-permute-start.16 = (f32[4,10,18,1]{3,2,1,0:T(8,128)S(1)}, f32[4,10,18,1]{3,2,1,0:T(8,128)S(1)}, u32[]{:S(2)}, u32[]{:S(2)}) collective-permute-start(f32[4,10,18,1]{3,2,1,0:T(8,128)S(1)} %get-tuple-element.27), channel_id=1, source_target_pairs={{1,0},{2,1},{3,2},{4,3},{5,4},{6,5},{7,6},{0,7},{9,8},{10,9},{11,1... | collective-permute-start | bytes 8648 | tf_op jit(solution)/shard_map/ppermute | solution.py:22
  98.9 5.8 collective-permute-start.17
  105.3 470.2 %copy-start.2 = (f32[4,8,16,128]{3,2,1,0:T(8,128)}, f32[4,8,16,128]{3,2,1,0:T(8,128)S(1)}, u32[]{:S(2)}) copy-start(f32[4,8,16,128]{3,2,1,0:T(8,128)S(1)} %fusion.15) | copy-start | bytes 786436
Sparse Core Ops, SparseCore 0:
  115.5 433.2 all-reduce.1
where the time goes:
time: 583 us; the launch traced here: 582 us
  waiting for transfers between devices  467 us (80%)
  starting transfers between devices  52 us (9%)
  other arithmetic  33.4 us (6%)
  between operations  14.5 us (2%)
  local copies, waits for them, and re-layouts  12.7 us (2%)
    psum x1, waiting for transfers between devices, local(): gram = lax.psum(local_gram, ('gx', 'gy', 'gz')) / count  433 us
    ppermute x9, starting transfers between devices, padded(): lax.ppermute(lax.slice_in_dim(block, 0, width, axis=dim), axis, backward)  32.1 us
    ppermute x9, waiting for transfers between devices, padded(): lax.ppermute(lax.slice_in_dim(block, 0, width, axis=dim), axis, backward)  25.5 us
    ppermute x9, starting transfers between devices, padded(): lax.ppermute(lax.slice_in_dim(block, block.shape[dim] - width, None, axis...  19.9 us
    another operation x3, other arithmetic, local(): lower = jnp.linalg.cholesky(gram)  12.4 us
  transfers between devices with their start and end apart: 19, of which 11 were waited for; matrix products, arithmetic and copies ran while one was open for 1% of the time, Pallas kernels for 0%

commit v1 on v0

--- a/solution.py
+++ b/solution.py
@@ -2,6 +2,7 @@
 import jax.numpy as jnp
 from jax import lax
 from jax.sharding import PartitionSpec as P
+from jax.lax import psum
 
 DT_STEP = 0.35
 VISCOSITY = 0.2
@@ -64,7 +65,7 @@
     local_gram = jnp.dot(
         stacked, stacked.T, precision=lax.Precision.HIGHEST, preferred_element_type=jnp.float32
     )
-    gram = lax.psum(local_gram, ("gx", "gy", "gz")) / count
+    gram = psum(psum(local_gram, ("gy", "gz")), axis_name="gx") / count
     lower = jnp.linalg.cholesky(gram)
     basis_next = jax.scipy.linalg.solve_triangular(lower, stacked, lower=True).reshape(
         modes + 1, 3, points

time: 583 us -> 403 us (0.69)
  the two profiles are of different devices: /device:TPU:1 before, /device:TPU:2 now
where the time goes in v1:
time: 403 us; the launch traced here: 402 us
  waiting for transfers between devices  293 us (73%)
  starting transfers between devices  46.1 us (11%)
  other arithmetic  33.4 us (8%)
  between operations  14.5 us (4%)
  local copies, waits for them, and re-layouts  12.7 us (3%)
    psum x2, waiting for transfers between devices, local(): gram = psum(psum(local_gram, ('gy', 'gz')), axis_name='gx') / count  252 us
    ppermute x9, starting transfers between devices, padded(): lax.ppermute(lax.slice_in_dim(block, 0, width, axis=dim), axis, backward)  26.1 us
    ppermute x9, waiting for transfers between devices, padded(): lax.ppermute(lax.slice_in_dim(block, 0, width, axis=dim), axis, backward)  20.7 us
    ppermute x9, waiting for transfers between devices, padded(): lax.ppermute(lax.slice_in_dim(block, block.shape[dim] - width, None, axis...  20.4 us
    ppermute x9, starting transfers between devices, padded(): lax.ppermute(lax.slice_in_dim(block, block.shape[dim] - width, None, axis...  19.7 us
    another operation x3, other arithmetic, local(): lower = jnp.linalg.cholesky(gram)  12.4 us
    another operation x1, other arithmetic, local(): jax.scipy.linalg.solve_triangular(lower, stacked, lower=True)  9.81 us
  transfers between devices with their start and end apart: 20, of which 16 were waited for; matrix products, arithmetic and copies ran while one was open for 1% of the time, Pallas kernels for 0%

profile of v1, /device:TPU:2, one launch (start us, length us, event | category | flops | bytes accessed | tf_op | source)
XLA Modules:
  0.0 402.5 jit_solution(10307079722030106917)
XLA Ops:
  8.3 3.4 collective-permute-start
  11.7 5.7 %collective-permute-start.1 = (f32[4,8,1,128]{3,2,1,0:T(1,128)S(1)}, f32[4,8,1,128]{3,2,1,0:T(1,128)S(1)}, u32[]{:S(2)}, u32[]{:S(2)}) collective-permute-start(f32[4,8,1,128]{3,2,1,0:T(1,128)S(1)} %get-tuple-element.68), channel_id=1, source_target_pairs={{8,0},{16,8},{24,16},{9,1},{17,9},{25,17},{10,2},{18,10},{26,18},{... | collective-permute-start | bytes 49160 | tf_op jit(solution)/shard_map/ppermute | solution.py:23
  19.6 9.9 %collective-permute-start.2 = (f32[4,1,18,128]{3,2,1,0:T(8,128)S(1)}, f32[4,1,18,128]{3,2,1,0:T(8,128)S(1)}, u32[]{:S(2)}, u32[]{:S(2)}) collective-permute-start(f32[4,1,18,128]{3,2,1,0:T(8,128)S(1)} %get-tuple-element.41), channel_id=1, source_target_pairs={{32,0},{64,32},{96,64},{128,96},{160,128},{192,160},{224,192},{256... | collective-permute-start | bytes 110600 | tf_op jit(solution)/shard_map/ppermute | solution.py:23
  29.5 1.9 collective-permute-start.3
  32.1 4.6 %collective-permute-done.3 = f32[4,1,18,128]{3,2,1,0:T(8,128)S(1)} collective-permute-done((f32[4,1,18,128]{3,2,1,0:T(8,128)S(1)}, f32[4,1,18,128]{3,2,1,0:T(8,128)S(1)}, u32[]{:S(2)}, u32[]{:S(2)}) %collective-permute-start.3) | collective-permute-done | bytes 36896 | tf_op jit(solution)/shard_map/ppermute | solution.py:20
  38.4 1.6 subtract_multiply_fusion.5
  40.0 4.3 %collective-permute-done.4 = f32[4,10,18,1]{3,2,1,0:T(8,128)S(1)} collective-permute-done((f32[4,10,18,1]{3,2,1,0:T(8,128)S(1)}, f32[4,10,18,1]{3,2,1,0:T(8,128)S(1)}, u32[]{:S(2)}, u32[]{:S(2)}) %collective-permute-start.4) | collective-permute-done | bytes 2912 | tf_op jit(solution)/shard_map/ppermute | solution.py:23
  44.3 3.3 collective-permute-done.5
  47.6 1.4 subtract_multiply_fusion.4
  49.0 1.5 fusion.24
  50.6 3.1 collective-permute-start.6
  53.7 2.7 collective-permute-start.7
  56.5 2.9 collective-permute-done.7
  59.4 1.9 collective-permute-start.8
  61.3 3.9 collective-permute-start.9
  65.3 3.1 collective-permute-done.9
  69.4 5.7 %collective-permute-done.10 = f32[4,10,18,1]{3,2,1,0:T(8,128)S(1)} collective-permute-done((f32[4,10,18,1]{3,2,1,0:T(8,128)S(1)}, f32[4,10,18,1]{3,2,1,0:T(8,128)S(1)}, u32[]{:S(2)}, u32[]{:S(2)}) %collective-permute-start.10) | collective-permute-done | bytes 2912 | tf_op jit(solution)/shard_map/ppermute | solution.py:23
  75.1 3.1 collective-permute-done.11
  78.9 1.9 collective-permute-start.12
  80.9 3.9 collective-permute-start.13
  85.0 1.5 collective-permute-done.13
  86.5 1.9 collective-permute-start.14
  88.4 3.9 collective-permute-start.15
  92.5 3.1 collective-permute-done.15
  96.5 5.7 %collective-permute-done.16 = f32[4,10,18,1]{3,2,1,0:T(8,128)S(1)} collective-permute-done((f32[4,10,18,1]{3,2,1,0:T(8,128)S(1)}, f32[4,10,18,1]{3,2,1,0:T(8,128)S(1)}, u32[]{:S(2)}, u32[]{:S(2)}) %collective-permute-start.16) | collective-permute-done | bytes 2912 | tf_op jit(solution)/shard_map/ppermute | solution.py:23
  102.3 3.1 collective-permute-done.17
  106.1 4.7 %copy.16 = f32[3,8,16,128]{0,3,2,1:T(8,128)} copy(f32[3,8,16,128]{3,2,1,0:T(8,128)S(1)} %slice.406) | data formatting | bytes 393216 | tf_op jit(solution)/shard_map/slice | solution.py:62
  110.8 4.1 %gather_fusion = f32[256,3]{1,0:T(8,128)S(1)} fusion(f32[3,16384]{0,1:T(8,128)} %bitcast.47, s32[1024]{0:T(1024)S(1)} %pad_clamp_fusion), kind=kCustom, calls=%fused_computation | custom fusion | bytes 7168 | tf_op jit(solution)/shard_map/jit(_take)/gather | solution.py:63
  116.6 116.8 %all-reduce.3.cloned.1.call-done = f32[128,128]{0,1:T(8,128)} async-done(((f32[128,128]{0,1:T(8,128)}), f32[128,128]{0,1:T(8,128)}) %all-reduce.3.cloned.1.call-update) | async-done | bytes 65552 | tf_op jit(solution)/shard_map/psum | solution.py:68
  233.6 135.4 %all-reduce.5.cloned.1.call-done = f32[128,128]{0,1:T(8,128)} async-done(((f32[128,128]{0,1:T(8,128)}), f32[128,128]{0,1:T(8,128)}) %all-reduce.5.cloned.1.call-update) | async-done | bytes 65552 | tf_op jit(solution)/shard_map/psum | solution.py:68
  370.8 11.7 %cholesky.16 = f32[128,128]{1,0:T(8,128)S(1)} custom-call(f32[128,128]{1,0:T(8,128)S(1)} %fusion.57), custom_call_target="Cholesky" | custom-call | tf_op jit(solution)/shard_map/jit(cholesky)/cholesky | solution.py:69
  383.8 9.8 %custom-call.7 = f32[1,128,128]{1,2,0:T(8,128)S(1)} custom-call(f32[1,128,128]{2,1,0:T(8,128)S(1)} %get-tuple-element.70), custom_call_target="InvertDiagBlocksLowerTriangular" | custom-call | tf_op jit(solution)/shard_map/jit(_solve_triangular)/triangular_solve | solution.py:70
  (74 shorter events, 16.3 us)
Async XLA Ops:
  7.2 43.3 %copy-start = (f32[4,8,16,128]{3,2,1,0:T(8,128)S(1)}, f32[4,8,16,128]{3,2,1,0:T(8,128)}, u32[]{:S(2)}) copy-start(f32[4,8,16,128]{3,2,1,0:T(8,128)} %param.6) | copy-start | bytes 786436
  7.2 49.3 %copy-start.4 = (s32[256]{0:T(256)S(1)}, s32[256]{0:T(256)}, u32[]{:S(2)}) copy-start(s32[256]{0:T(256)} %param.8) | copy-start | bytes 3076
  7.2 226.2 %all-reduce.3.cloned.1.call-start = ((), (), s32[]{:S(2)}) async-start(), calls=%async_computation | async-start | bytes 131072 | tf_op jit(solution)/shard_map/psum | solution.py:68
  8.3 10.0 %collective-permute-start = (f32[4,8,1,128]{3,2,1,0:T(1,128)S(1)}, f32[4,8,1,128]{3,2,1,0:T(1,128)S(1)}, u32[]{:S(2)}, u32[]{:S(2)}) collective-permute-start(f32[4,8,1,128]{3,2,1,0:T(1,128)S(1)} %get-tuple-element.67), channel_id=1, source_target_pairs={{0,8},{8,16},{16,24},{1,9},{9,17},{17,25},{2,10},{10,18},{18,26},{... | collective-permute-start | bytes 49160 | tf_op jit(solution)/shard_map/ppermute | solution.py:20
  11.7 7.1 %collective-permute-start.1 = (f32[4,8,1,128]{3,2,1,0:T(1,128)S(1)}, f32[4,8,1,128]{3,2,1,0:T(1,128)S(1)}, u32[]{:S(2)}, u32[]{:S(2)}) collective-permute-start(f32[4,8,1,128]{3,2,1,0:T(1,128)S(1)} %get-tuple-element.68), channel_id=1, source_target_pairs={{8,0},{16,8},{24,16},{9,1},{17,9},{25,17},{10,2},{18,10},{26,18},{... | collective-permute-start | bytes 49160 | tf_op jit(solution)/shard_map/ppermute | solution.py:23
  19.6 12.5 %collective-permute-start.2 = (f32[4,1,18,128]{3,2,1,0:T(8,128)S(1)}, f32[4,1,18,128]{3,2,1,0:T(8,128)S(1)}, u32[]{:S(2)}, u32[]{:S(2)}) collective-permute-start(f32[4,1,18,128]{3,2,1,0:T(8,128)S(1)} %get-tuple-element.41), channel_id=1, source_target_pairs={{32,0},{64,32},{96,64},{128,96},{160,128},{192,160},{224,192},{256... | collective-permute-start | bytes 110600 | tf_op jit(solution)/shard_map/ppermute | solution.py:23
  29.5 7.2 %collective-permute-start.3 = (f32[4,1,18,128]{3,2,1,0:T(8,128)S(1)}, f32[4,1,18,128]{3,2,1,0:T(8,128)S(1)}, u32[]{:S(2)}, u32[]{:S(2)}) collective-permute-start(f32[4,1,18,128]{3,2,1,0:T(8,128)S(1)} %get-tuple-element.40), channel_id=1, source_target_pairs={{0,32},{32,64},{64,96},{96,128},{128,160},{160,192},{192,224},{224... | collective-permute-start | bytes 110600 | tf_op jit(solution)/shard_map/ppermute | solution.py:20
  37.7 40.9 %copy-start.3 = (f32[3]{0:T(128)S(1)}, f32[3]{0:T(128)}, u32[]{:S(2)}) copy-start(f32[3]{0:T(128)} %constant.80.clone) | copy-start | bytes 40
  37.9 6.4 %collective-permute-start.4 = (f32[4,10,18,1]{3,2,1,0:T(8,128)S(1)}, f32[4,10,18,1]{3,2,1,0:T(8,128)S(1)}, u32[]{:S(2)}, u32[]{:S(2)}) collective-permute-start(f32[4,10,18,1]{3,2,1,0:T(8,128)S(1)} %get-tuple-element.31), channel_id=1, source_target_pairs={{1,0},{2,1},{3,2},{4,3},{5,4},{6,5},{7,6},{0,7},{9,8},{10,9},{11,1... | collective-permute-start | bytes 8648 | tf_op jit(solution)/shard_map/ppermute | solution.py:23
  37.9 9.6 %collective-permute-start.5 = (f32[4,10,18,1]{3,2,1,0:T(8,128)S(1)}, f32[4,10,18,1]{3,2,1,0:T(8,128)S(1)}, u32[]{:S(2)}, u32[]{:S(2)}) collective-permute-start(f32[4,10,18,1]{3,2,1,0:T(8,128)S(1)} %get-tuple-element.32), channel_id=1, source_target_pairs={{0,1},{1,2},{2,3},{3,4},{4,5},{5,6},{6,7},{7,0},{8,9},{9,10},{10,1... | collective-permute-start | bytes 8648 | tf_op jit(solution)/shard_map/ppermute | solution.py:20
  40.0 44.8 %copy-start.1 = (f32[127,3,256]{2,0,1:T(8,128)S(1)}, f32[127,3,256]{2,0,1:T(8,128)}, u32[]{:S(2)}) copy-start(f32[127,3,256]{2,0,1:T(8,128)} %param.7) | copy-start | bytes 1170436
  50.6 5.9 %collective-permute-start.6 = (f32[4,8,1,128]{3,2,1,0:T(1,128)S(1)}, f32[4,8,1,128]{3,2,1,0:T(1,128)S(1)}, u32[]{:S(2)}, u32[]{:S(2)}) collective-permute-start(f32[4,8,1,128]{3,2,1,0:T(1,128)S(1)} %get-tuple-element.58), channel_id=1, source_target_pairs={{0,8},{8,16},{16,24},{1,9},{9,17},{17,25},{2,10},{10,18},{18,26},{... | collective-permute-start | bytes 49160 | tf_op jit(solution)/shard_map/ppermute | solution.py:20
  53.7 5.6 %collective-permute-start.7 = (f32[4,8,1,128]{3,2,1,0:T(1,128)S(1)}, f32[4,8,1,128]{3,2,1,0:T(1,128)S(1)}, u32[]{:S(2)}, u32[]{:S(2)}) collective-permute-start(f32[4,8,1,128]{3,2,1,0:T(1,128)S(1)} %get-tuple-element.59), channel_id=1, source_target_pairs={{8,0},{16,8},{24,16},{9,1},{17,9},{25,17},{10,2},{18,10},{26,18},{... | collective-permute-start | bytes 49160 | tf_op jit(solution)/shard_map/ppermute | solution.py:23
  59.4 6.0 %collective-permute-start.8 = (f32[4,1,18,128]{3,2,1,0:T(8,128)S(1)}, f32[4,1,18,128]{3,2,1,0:T(8,128)S(1)}, u32[]{:S(2)}, u32[]{:S(2)}) collective-permute-start(f32[4,1,18,128]{3,2,1,0:T(8,128)S(1)} %get-tuple-element.38), channel_id=1, source_target_pairs={{32,0},{64,32},{96,64},{128,96},{160,128},{192,160},{224,192},{256... | collective-permute-start | bytes 110600 | tf_op jit(solution)/shard_map/ppermute | solution.py:23
  61.3 7.2 %collective-permute-start.9 = (f32[4,1,18,128]{3,2,1,0:T(8,128)S(1)}, f32[4,1,18,128]{3,2,1,0:T(8,128)S(1)}, u32[]{:S(2)}, u32[]{:S(2)}) collective-permute-start(f32[4,1,18,128]{3,2,1,0:T(8,128)S(1)} %get-tuple-element.37), channel_id=1, source_target_pairs={{0,32},{32,64},{64,96},{96,128},{128,160},{160,192},{192,224},{224... | collective-permute-start | bytes 110600 | tf_op jit(solution)/shard_map/ppermute | solution.py:20
  68.7 6.4 %collective-permute-start.10 = (f32[4,10,18,1]{3,2,1,0:T(8,128)S(1)}, f32[4,10,18,1]{3,2,1,0:T(8,128)S(1)}, u32[]{:S(2)}, u32[]{:S(2)}) collective-permute-start(f32[4,10,18,1]{3,2,1,0:T(8,128)S(1)} %get-tuple-element.29), channel_id=1, source_target_pairs={{1,0},{2,1},{3,2},{4,3},{5,4},{6,5},{7,6},{0,7},{9,8},{10,9},{11,1... | collective-permute-start | bytes 8648 | tf_op jit(solution)/shard_map/ppermute | solution.py:23
  68.8 9.5 %collective-permute-start.11 = (f32[4,10,18,1]{3,2,1,0:T(8,128)S(1)}, f32[4,10,18,1]{3,2,1,0:T(8,128)S(1)}, u32[]{:S(2)}, u32[]{:S(2)}) collective-permute-start(f32[4,10,18,1]{3,2,1,0:T(8,128)S(1)} %get-tuple-element.30), channel_id=1, source_target_pairs={{0,1},{1,2},{2,3},{3,4},{4,5},{5,6},{6,7},{7,0},{8,9},{9,10},{10,1... | collective-permute-start | bytes 8648 | tf_op jit(solution)/shard_map/ppermute | solution.py:20
  78.9 6.1 %collective-permute-start.12 = (f32[4,8,1,128]{3,2,1,0:T(1,128)S(1)}, f32[4,8,1,128]{3,2,1,0:T(1,128)S(1)}, u32[]{:S(2)}, u32[]{:S(2)}) collective-permute-start(f32[4,8,1,128]{3,2,1,0:T(1,128)S(1)} %get-tuple-element.49), channel_id=1, source_target_pairs={{0,8},{8,16},{16,24},{1,9},{9,17},{17,25},{2,10},{10,18},{18,26},{... | collective-permute-start | bytes 49160 | tf_op jit(solution)/shard_map/ppermute | solution.py:20
  80.9 5.6 %collective-permute-start.13 = (f32[4,8,1,128]{3,2,1,0:T(1,128)S(1)}, f32[4,8,1,128]{3,2,1,0:T(1,128)S(1)}, u32[]{:S(2)}, u32[]{:S(2)}) collective-permute-start(f32[4,8,1,128]{3,2,1,0:T(1,128)S(1)} %get-tuple-element.50), channel_id=1, source_target_pairs={{8,0},{16,8},{24,16},{9,1},{17,9},{25,17},{10,2},{18,10},{26,18},{... | collective-permute-start | bytes 49160 | tf_op jit(solution)/shard_map/ppermute | solution.py:23
  86.5 6.0 %collective-permute-start.14 = (f32[4,1,18,128]{3,2,1,0:T(8,128)S(1)}, f32[4,1,18,128]{3,2,1,0:T(8,128)S(1)}, u32[]{:S(2)}, u32[]{:S(2)}) collective-permute-start(f32[4,1,18,128]{3,2,1,0:T(8,128)S(1)} %get-tuple-element.35), channel_id=1, source_target_pairs={{32,0},{64,32},{96,64},{128,96},{160,128},{192,160},{224,192},{256... | collective-permute-start | bytes 110600 | tf_op jit(solution)/shard_map/ppermute | solution.py:23
  88.4 7.2 %collective-permute-start.15 = (f32[4,1,18,128]{3,2,1,0:T(8,128)S(1)}, f32[4,1,18,128]{3,2,1,0:T(8,128)S(1)}, u32[]{:S(2)}, u32[]{:S(2)}) collective-permute-start(f32[4,1,18,128]{3,2,1,0:T(8,128)S(1)} %get-tuple-element.34), channel_id=1, source_target_pairs={{0,32},{32,64},{64,96},{96,128},{128,160},{160,192},{192,224},{224... | collective-permute-start | bytes 110600 | tf_op jit(solution)/shard_map/ppermute | solution.py:20
  95.9 6.4 %collective-permute-start.16 = (f32[4,10,18,1]{3,2,1,0:T(8,128)S(1)}, f32[4,10,18,1]{3,2,1,0:T(8,128)S(1)}, u32[]{:S(2)}, u32[]{:S(2)}) collective-permute-start(f32[4,10,18,1]{3,2,1,0:T(8,128)S(1)} %get-tuple-element.27), channel_id=1, source_target_pairs={{1,0},{2,1},{3,2},{4,3},{5,4},{6,5},{7,6},{0,7},{9,8},{10,9},{11,1... | collective-permute-start | bytes 8648 | tf_op jit(solution)/shard_map/ppermute | solution.py:23
  95.9 9.5 %collective-permute-start.17 = (f32[4,10,18,1]{3,2,1,0:T(8,128)S(1)}, f32[4,10,18,1]{3,2,1,0:T(8,128)S(1)}, u32[]{:S(2)}, u32[]{:S(2)}) collective-permute-start(f32[4,10,18,1]{3,2,1,0:T(8,128)S(1)} %get-tuple-element.28), channel_id=1, source_target_pairs={{0,1},{1,2},{2,3},{3,4},{4,5},{5,6},{6,7},{7,0},{8,9},{9,10},{10,1... | collective-permute-start | bytes 8648 | tf_op jit(solution)/shard_map/ppermute | solution.py:20
  106.0 289.6 %copy-start.2 = (f32[4,8,16,128]{3,2,1,0:T(8,128)}, f32[4,8,16,128]{3,2,1,0:T(8,128)S(1)}, u32[]{:S(2)}) copy-start(f32[4,8,16,128]{3,2,1,0:T(8,128)S(1)} %fusion.15) | copy-start | bytes 786436
  116.1 252.8 %all-reduce.5.cloned.1.call-start = ((), (), s32[]{:S(2)}) async-start(), calls=%async_computation.1 | async-start | bytes 131072 | tf_op jit(solution)/shard_map/psum | solution.py:68
Sparse Core Ops, SparseCore 0:
  116.2 117.0 all-reduce.2
  235.8 133.1 all-reduce.4
